TPU v7x, 128 devices: a whole 4x4x4 slice. The times are simulated.
128 devices in a mesh: blk: 16 (over z_lo, x, core), narrow: 8 (over z_hi, y).
Axes of the slice: x: 4, y: 4, z: 4 (z_hi: 2, z_lo: 2; z = z_hi * 2 + z_lo), core: 2. Of those that a mesh axis runs over, the one named last changes fastest.
Arguments:
- codes: bfloat16 [24576, 12288], P(('blk', 'narrow')), may hold values from -24 to 24
- signals: bfloat16 [24576, 192], P(('blk', 'narrow')), may hold values from -6 to 6
- dictionary: bfloat16 [12288, 192], P('blk'), may hold values from -0.0546875 to 0.0546875
Outputs:
- new_codes: bfloat16 [24576, 12288], P(('blk', 'narrow'))
- dict_grad: float32 [12288, 192], P(('blk', 'narrow'))
All inputs are finite; a program needn't handle non-finite values.
Results may differ from a plain program's by a relative error of at most 0.0095.
Values may be sent and summed in bfloat16 or wider, within the bound.
No kernel may reach another device: no remote copies, remote signals or barrier semaphores. Data moves between devices by JAX's collectives and lax.ppermute only.
A program may use at most 64 MiB of HBM per device.

v0:
```python
import functools

import jax
import jax.numpy as jnp
from jax import lax
from jax.experimental import pallas as pl
from jax.experimental.pallas import tpu as pltpu
from jax.sharding import Mesh
from jax.sharding import PartitionSpec as P


AXES = ("z_lo", "x", "core", "z_hi", "y")
SIZES = (2, 4, 2, 2, 4)
ANY = pl.BlockSpec(memory_space=pl.ANY)
SMEM = pl.BlockSpec(memory_space=pltpu.SMEM)
VMEM = pl.BlockSpec(memory_space=pltpu.VMEM)
F32, BF16 = jnp.float32, jnp.bfloat16
PARAMS = pltpu.CompilerParams(vmem_limit_bytes=24 << 20)


def near_memory(value):
    return pltpu.with_memory_space_constraint(value, pltpu.VMEM)


def far_memory(value):
    return pltpu.with_memory_space_constraint(value, pltpu.HBM)


def send(value, dx, dz):
    def index(z, x, c):
        return (((z % 2) * 4 + x) * 2 + c) * 2 + z // 2

    pairs = []
    for z in range(4):
        for x in range(4):
            for c, way in ((0, 1), (1, -1)):
                pairs.append((index(z, x, c), index((z + way * dz) % 4, (x + way * dx) % 4, c)))
    return lax.ppermute(value, ("z_lo", "x", "core", "z_hi"), pairs)


def send_core(value):
    return lax.ppermute(value, "core", [(0, 1), (1, 0)])


def columns(block, width):
    return pl.ds(pl.multiple_of(block * width, 128), width)


def chunk_place(shift, core, x, z_lo):
    dz, dx = shift
    return ((z_lo[0] + dz) % 2) * 4 + (x[0] + 4 + dx * (1 - 2 * core[0])) % 4


def take_kernel(flip, core, x, z_lo, codes, out, sems):
    width = out.shape[1] // 8
    half = 1 - core[0] if flip else core[0]
    copies = []
    for q in range(8):
        source = codes.at[:, columns(2 * q + half, width)]
        copies.append(pltpu.make_async_copy(source, out.at[:, columns(q, width)], sems.at[q]))
    for copy in copies:
        copy.start()
    for copy in copies:
        copy.wait()


def take_half(flip, core, x, z_lo, codes):
    rows, atom_count = codes.shape
    return pl.pallas_call(
        functools.partial(take_kernel, flip),
        out_shape=pltpu.VMEM((rows, atom_count // 2), BF16),
        in_specs=[SMEM, SMEM, SMEM, ANY],
        out_specs=VMEM,
        scratch_shapes=[pltpu.SemaphoreType.DMA((8,))],
        compiler_params=PARAMS,
        name="take",
    )(core, x, z_lo, far_memory(codes))


def along_atoms(left, right):
    return lax.dot_general(left, right, (((1,), (1,)), ((), ())), preferred_element_type=F32)


def whole(pieces):
    values = [piece[...] for piece in pieces]
    return values[0] if len(values) == 1 else jnp.concatenate(values, axis=0)


def take(refs, counts):
    parts, at = [], 0
    for count in counts:
        parts.append(refs[at : at + count])
        at += count
    return parts, refs[at:]


def estimate_kernel(shifts, counts, has_start, core, x, z_lo, own, other, *refs):
    start = refs[0] if has_start else None
    parts, rest = take(refs[1:] if has_start else refs, counts)
    (out,) = rest
    rows = own.shape[0]
    width = own.shape[1] // 8
    for k, pieces in enumerate(parts):
        atoms = whole(pieces)
        span = columns(chunk_place(shifts[k], core, x, z_lo), width)
        for low, source in ((0, own), (rows, other)):
            term = along_atoms(source[:, span], atoms)
            if k:
                out[low : low + rows] += term
            elif has_start:
                out[low : low + rows] = start[low : low + rows] + term
            else:
                out[low : low + rows] = term


def estimate(core, x, z_lo, own, other, start, shifts, parts):
    rows = own.shape[0]
    features = sum(p.shape[0] for p in parts[0])
    counts = tuple(len(p) for p in parts)
    flat = [p for pieces in parts for p in pieces]
    given = [own, other] + ([] if start is None else [start]) + flat
    return pl.pallas_call(
        functools.partial(estimate_kernel, shifts, counts, start is not None),
        out_shape=pltpu.VMEM((2 * rows, features), F32),
        in_specs=[SMEM] * 3 + [VMEM] * len(given),
        out_specs=VMEM,
        compiler_params=PARAMS,
        name="estimate",
    )(core, x, z_lo, *[near_memory(v) for v in given])


def misfit_of(mine, theirs, signal_own, signal_other):
    rows = signal_own.shape[0]
    first = mine[0:rows] + theirs[rows : 2 * rows] - signal_own[...].astype(F32)
    second = mine[rows : 2 * rows] + theirs[0:rows] - signal_other[...].astype(F32)
    return jnp.concatenate([first.astype(BF16), second.astype(BF16)], axis=0)


def update_kernel(shifts, counts, core, x, z_lo, own, other, mine, theirs, signal_own, signal_other, *refs):
    parts, rest = take(refs, counts)
    fresh_own, fresh_other, out, codes_out, back, sems = rest
    copies = []
    rows = own.shape[0]
    width = own.shape[1] // 8
    misfit = misfit_of(mine, theirs, signal_own, signal_other)
    for k, pieces in enumerate(parts):
        atoms = whole(pieces)
        span = columns(chunk_place(shifts[k], core, x, z_lo), width)
        for low, source, target in ((0, own, fresh_own), (rows, other, fresh_other)):
            correlation = jnp.dot(misfit[low : low + rows], atoms, preferred_element_type=F32)
            value = source[:, span].astype(F32) - 4.0 * correlation
            fresh = (value - jnp.clip(value, -0.5, 0.5)).astype(BF16)
            target[:, span] = fresh
            if target is fresh_own:
                block = 2 * chunk_place(shifts[k], core, x, z_lo) + core[0]
                copy = pltpu.make_async_copy(target.at[:, span], codes_out.at[:, columns(block, width)], sems.at[0, k])
            else:
                copy = pltpu.make_async_copy(target.at[:, span], back.at[:, span], sems.at[1, k])
            copy.start()
            copies.append(copy)
            term = along_atoms(fresh, atoms)
            if k:
                out[low : low + rows] += term
            else:
                out[low : low + rows] = term
    for copy in copies:
        copy.wait()


def update(core, x, z_lo, own, other, mine, theirs, signal_own, signal_other, shifts, parts):
    rows = own.shape[0]
    features = sum(p.shape[0] for p in parts[0])
    counts = tuple(len(p) for p in parts)
    flat = [p for pieces in parts for p in pieces]
    given = [own, other, mine, theirs, signal_own, signal_other] + flat
    return pl.pallas_call(
        functools.partial(update_kernel, shifts, counts),
        out_shape=(
            pltpu.VMEM(own.shape, BF16),
            pltpu.VMEM(own.shape, BF16),
            pltpu.VMEM((2 * rows, features), F32),
            pltpu.HBM((rows, 2 * own.shape[1]), BF16),
            pltpu.HBM(own.shape, BF16),
        ),
        in_specs=[SMEM] * 3 + [VMEM] * len(given),
        out_specs=(VMEM,) * 3 + (ANY, ANY),
        scratch_shapes=[pltpu.SemaphoreType.DMA((2, len(parts)))],
        compiler_params=PARAMS,
        name="update",
    )(core, x, z_lo, *[near_memory(v) for v in given])


def gradient_kernel(mine, theirs, signal_own, signal_other, own, other, out, buf, sems):
    width = own.shape[1] // 8
    copies = []
    misfit = misfit_of(mine, theirs, signal_own, signal_other)
    wide = jnp.concatenate([misfit, misfit[:, 128:192]], axis=1)
    part = width // 8
    low = lax.broadcasted_iota(jnp.int32, (part // 2, 128), 1) < 64
    for q in range(8):
        span = slice(q * width, (q + 1) * width)
        codes = jnp.concatenate([own[:, span], other[:, span]], axis=0)
        product = lax.dot_general(codes, wide, (((0,), (0,)), ((), ())), preferred_element_type=F32)
        for n in range(8):
            piece = product[n * part : (n + 1) * part]
            buf[q * 8 + n, 0:part] = piece[:, 0:128].astype(BF16)
            tail = jnp.where(low, piece[: part // 2, 128:256], piece[part // 2 :, 128:256])
            buf[q * 8 + n, part : part + part // 2] = tail.astype(BF16)
        copy = pltpu.make_async_copy(buf.at[q * 8 : q * 8 + 8], out.at[q * 8 : q * 8 + 8], sems.at[q])
        copy.start()
        copies.append(copy)
    for copy in copies:
        copy.wait()


def gradient(mine, theirs, signal_own, signal_other, own, other):
    part = own.shape[1] // 64
    given = [mine, theirs, signal_own, signal_other, own, other]
    pieces = (64, part + part // 2, 128)
    return pl.pallas_call(
        gradient_kernel,
        out_shape=pltpu.HBM(pieces, BF16),
        in_specs=[VMEM] * 6,
        out_specs=ANY,
        scratch_shapes=[pltpu.VMEM(pieces, BF16), pltpu.SemaphoreType.DMA((8,))],
        compiler_params=PARAMS,
        name="gradient",
    )(*[near_memory(v) for v in given])


def place_kernel(core, fresh_back, codes, codes_out, sems):
    width = fresh_back.shape[1] // 8
    copies = []
    for q in range(8):
        target = codes_out.at[:, columns(2 * q + 1 - core[0], width)]
        copies.append(pltpu.make_async_copy(fresh_back.at[:, columns(q, width)], target, sems.at[q]))
    for copy in copies:
        copy.start()
    for copy in copies:
        copy.wait()


def place(core, fresh_back, codes):
    return pl.pallas_call(
        place_kernel,
        out_shape=pltpu.HBM(codes.shape, BF16),
        in_specs=[SMEM, VMEM, ANY],
        out_specs=ANY,
        scratch_shapes=[pltpu.SemaphoreType.DMA((8,))],
        input_output_aliases={2: 0},
        compiler_params=PARAMS,
        name="place",
    )(core, near_memory(fresh_back), far_memory(codes))


def finish_kernel(scale, pieces, grad_out):
    part = grad_out.shape[0]
    total = pieces[0].astype(F32)
    for i in range(1, pieces.shape[0]):
        total = total + pieces[i].astype(F32)
    total = total * scale
    grad_out[:, 0:128] = total[0:part]
    grad_out[0 : part // 2, 128:192] = total[part:, 0:64]
    grad_out[part // 2 :, 128:192] = total[part:, 64:128]


def finish(scale, pieces, grad_shape):
    return pl.pallas_call(
        functools.partial(finish_kernel, scale),
        out_shape=jax.ShapeDtypeStruct(grad_shape, F32),
        in_specs=[VMEM],
        out_specs=VMEM,
        compiler_params=PARAMS,
        name="finish",
    )(near_memory(pieces))


def step(codes, signals, dictionary):
    rows, atom_count = codes.shape
    core, x, z_lo = (lax.axis_index(a).astype(jnp.int32).reshape(1) for a in ("core", "x", "z_lo"))
    atoms = dictionary.T
    side = send(atoms, 1, 0)
    near = send(atoms, 0, 1)
    reverse = send(atoms, -1, 0)
    away = take_half(True, core, x, z_lo, codes)
    other = send_core(away)
    own = take_half(False, core, x, z_lo, codes)
    signal_other = send_core(signals)
    far = send(side, 1, 0)
    near_far = send(side, 1, 1)
    near_side = send(atoms, 1, 1)
    near_reverse = send(reverse, 0, 1)
    plan = [
        ((0, 0), (atoms,)),
        ((0, -1), (side,)),
        ((0, 1), (reverse,)),
        ((1, 0), (near,)),
        ((0, 2), (far,)),
        ((1, 2), (near_far,)),
        ((1, -1), (near_side,)),
        ((1, 1), (near_reverse,)),
    ]
    shifts = [p[0] for p in plan]
    parts = [p[1] for p in plan]
    mine = None
    for first, last in ((0, 4), (4, 7), (7, 8)):
        mine = estimate(core, x, z_lo, own, other, mine, shifts[first:last], parts[first:last])
    theirs = send_core(mine)
    fresh_own, fresh_other, second, fresh, back = update(
        core, x, z_lo, own, other, mine, theirs, signals, signal_other, shifts, parts
    )
    second_theirs = send_core(second)
    fresh_back = send_core(back)
    pieces = gradient(second, second_theirs, signals, signal_other, fresh_own, fresh_other)
    pieces = functools.partial(lax.all_to_all, tiled=True)(pieces, ("z_lo", "x", "z_hi", "y"), 0, 0)
    fresh = place(core, fresh_back, fresh)
    total_rows = rows
    for size in SIZES:
        total_rows *= size
    grad_shape = (atom_count // 128, signals.shape[1])
    return fresh, finish(float(total_rows) ** -0.5, pieces, grad_shape)


def solution(mesh):
    fine = Mesh(mesh.devices.reshape(SIZES), AXES)
    every = P(AXES, None)
    return jax.shard_map(
        step,
        mesh=fine,
        in_specs=(every, every, P(("z_lo", "x", "core"), None)),
        out_specs=(every, every),
        check_vma=False,
    )
```

profile of v0, /device:TPU:0, one launch (start us, length us, event | category | flops | bytes accessed | tf_op | source)
XLA Modules:
  0.0 78.8 jit_solution(16253797083628097384)
XLA Ops:
  0.6 1.7 %take.3 = bf16[192,6144]{1,0:T(8,128)(2,1)S(1)} custom-call(s32[1]{0:T(128)} %bitcast.core, s32[1]{0:T(128)} %bitcast.1.x, s32[1]{0:T(128)} %bitcast.2.z_lo, bf16[192,12288]{1,0:T(8,128)(2,1)} %codes.3), custom_call_target="tpu_custom_call" | custom-call | tf_op jit(solution)/shard_map/take/pallas_call | solution.py:69
  2.5 1.7 %collective-permute-start.1 = (bf16[192,768]{1,0:T(8,128)(2,1)S(1)}, bf16[192,768]{1,0:T(8,128)(2,1)S(1)}, u32[]{:S(2)}, u32[]{:S(2)}) collective-permute-start(bf16[192,768]{1,0:T(8,128)(2,1)S(1)} %bitcast.4), channel_id=1, source_target_pairs={{0,16},{8,56},{16,32},{24,8},{32,48},{40,24},{48,0},{56,40},{64,80... | collective-permute-start | bytes 884744 | tf_op jit(solution)/shard_map/ppermute | solution.py:38
  4.1 1.9 %collective-permute-start.3 = (bf16[192,768]{1,0:T(8,128)(2,1)S(1)}, bf16[192,768]{1,0:T(8,128)(2,1)S(1)}, u32[]{:S(2)}, u32[]{:S(2)}) collective-permute-start(bf16[192,768]{1,0:T(8,128)(2,1)S(1)} %bitcast.5), channel_id=1, source_target_pairs={{0,64},{8,76},{16,80},{24,92},{32,96},{40,108},{48,112},{56,124},{... | collective-permute-start | bytes 884744 | tf_op jit(solution)/shard_map/ppermute | solution.py:38
  6.1 1.7 %collective-permute-start.2 = (bf16[192,768]{1,0:T(8,128)(2,1)S(1)}, bf16[192,768]{1,0:T(8,128)(2,1)S(1)}, u32[]{:S(2)}, u32[]{:S(2)}) collective-permute-start(bf16[192,768]{1,0:T(8,128)(2,1)S(1)} %bitcast.6), channel_id=1, source_target_pairs={{0,48},{8,24},{16,0},{24,40},{32,16},{40,56},{48,32},{56,8},{64,11... | collective-permute-start | bytes 884744 | tf_op jit(solution)/shard_map/ppermute | solution.py:38
  7.8 1.6 %collective-permute-start.6 = (bf16[192,768]{1,0:T(8,128)(2,1)S(1)}, bf16[192,768]{1,0:T(8,128)(2,1)S(1)}, u32[]{:S(2)}, u32[]{:S(2)}) collective-permute-start(bf16[192,768]{1,0:T(8,128)(2,1)S(1)} %bitcast.7), channel_id=1, source_target_pairs={{0,80},{8,124},{16,96},{24,76},{32,112},{40,92},{48,64},{56,108},{... | collective-permute-start | bytes 884744 | tf_op jit(solution)/shard_map/ppermute | solution.py:38
  9.4 1.0 %collective-permute-done.1.refs_1_ = bf16[192,768]{1,0:T(8,128)(2,1)S(1)} collective-permute-done((bf16[192,768]{1,0:T(8,128)(2,1)S(1)}, bf16[192,768]{1,0:T(8,128)(2,1)S(1)}, u32[]{:S(2)}, u32[]{:S(2)}) %collective-permute-start.1) | collective-permute-done | bytes 294944 | tf_op jit(solution)/shard_map/ppermute | solution.py:38
  10.5 4.2 %collective-permute-start.5 = (bf16[192,768]{1,0:T(8,128)(2,1)S(1)}, bf16[192,768]{1,0:T(8,128)(2,1)S(1)}, u32[]{:S(2)}, u32[]{:S(2)}) collective-permute-start(bf16[192,768]{1,0:T(8,128)(2,1)S(1)} %collective-permute-done.1.refs_1_), channel_id=1, source_target_pairs={{0,80},{8,124},{16,96},{24,76},{32,112},{40,92},{48,64},{56,108},{... | collective-permute-start | bytes 884744 | tf_op jit(solution)/shard_map/ppermute | solution.py:38
  14.7 1.9 %collective-permute-start.4 = (bf16[192,768]{1,0:T(8,128)(2,1)S(1)}, bf16[192,768]{1,0:T(8,128)(2,1)S(1)}, u32[]{:S(2)}, u32[]{:S(2)}) collective-permute-start(bf16[192,768]{1,0:T(8,128)(2,1)S(1)} %collective-permute-done.1.refs_1_), channel_id=1, source_target_pairs={{0,16},{8,56},{16,32},{24,8},{32,48},{40,24},{48,0},{56,40},{64,80... | collective-permute-start | bytes 884744 | tf_op jit(solution)/shard_map/ppermute | solution.py:38
  16.6 1.9 %collective-permute-start.7 = (bf16[192,768]{1,0:T(8,128)(2,1)S(1)}, bf16[192,768]{1,0:T(8,128)(2,1)S(1)}, u32[]{:S(2)}, u32[]{:S(2)}) collective-permute-start(bf16[192,768]{1,0:T(8,128)(2,1)S(1)} %collective-permute-done.2.refs_2_), channel_id=1, source_target_pairs={{0,64},{8,76},{16,80},{24,92},{32,96},{40,108},{48,112},{56,124},{... | collective-permute-start | bytes 884744 | tf_op jit(solution)/shard_map/ppermute | solution.py:38
  18.5 1.7 %take.2.own = bf16[192,6144]{1,0:T(8,128)(2,1)S(1)} custom-call(s32[1]{0:T(128)} %bitcast.core, s32[1]{0:T(128)} %bitcast.1.x, s32[1]{0:T(128)} %bitcast.2.z_lo, bf16[192,12288]{1,0:T(8,128)(2,1)} %codes.3), custom_call_target="tpu_custom_call" | custom-call | tf_op jit(solution)/shard_map/take/pallas_call | solution.py:69
  20.2 0.8 %estimate.3.refs_0_ = f32[384,192]{1,0:T(8,128)S(1)} custom-call(s32[1]{0:T(128)} %bitcast.core, s32[1]{0:T(128)} %bitcast.1.x, s32[1]{0:T(128)} %bitcast.2.z_lo, bf16[192,6144]{1,0:T(8,128)(2,1)S(1)} %take.2.own, bf16[192,6144]{1,0:T(8,128)(2,1)S(1)} %collective-permute-done.other, bf16[192,768]{1,0:T(8,128)(2,1)S(1)} %bitcast.8, ...), custom_call_target="tpu_custom_call" | custom-call | tf_op jit(solution)/shard_map/estimate/pallas_call | solution.py:122
  21.0 2.6 %collective-permute-done.5.refs_2_.refs_5_ = bf16[192,768]{1,0:T(8,128)(2,1)S(1)} collective-permute-done((bf16[192,768]{1,0:T(8,128)(2,1)S(1)}, bf16[192,768]{1,0:T(8,128)(2,1)S(1)}, u32[]{:S(2)}, u32[]{:S(2)}) %collective-permute-start.5) | collective-permute-done | bytes 294944 | tf_op jit(solution)/shard_map/ppermute | solution.py:38
  23.6 2.1 %collective-permute-done.4.refs_1_.refs_4_ = bf16[192,768]{1,0:T(8,128)(2,1)S(1)} collective-permute-done((bf16[192,768]{1,0:T(8,128)(2,1)S(1)}, bf16[192,768]{1,0:T(8,128)(2,1)S(1)}, u32[]{:S(2)}, u32[]{:S(2)}) %collective-permute-start.4) | collective-permute-done | bytes 294944 | tf_op jit(solution)/shard_map/ppermute | solution.py:38
  25.8 0.7 estimate.4.refs_0_
  26.7 0.3 estimate.5.mine
  27.6 1.4 %collective-permute-done.9.signal_other = bf16[192,192]{1,0:T(8,128)(2,1)S(1)} collective-permute-done((bf16[192,192]{1,0:T(8,128)(2,1)S(1)}, bf16[192,192]{1,0:T(8,128)(2,1)S(1)}, u32[]{:S(2)}, u32[]{:S(2)}) %collective-permute-start.9) | collective-permute-done | bytes 73760 | tf_op jit(solution)/shard_map/ppermute | solution.py:42
  29.0 3.7 %update.1 = (bf16[192,6144]{1,0:T(8,128)(2,1)S(1)}, bf16[192,6144]{1,0:T(8,128)(2,1)S(1)}, f32[384,192]{1,0:T(8,128)S(1)}, bf16[192,12288]{1,0:T(8,128)(2,1)}, bf16[192,6144]{1,0:T(8,128)(2,1)}) custom-call(s32[1]{0:T(128)} %bitcast.core, s32[1]{0:T(128)} %bitcast.1.x, s32[1]{0:T(128)} %bitcast.2.z_lo, bf16[192,6144]{1,0:T(8,128)(2,1)S(1)} %take.2.own, ...), custom_call_target="tpu_custom_call" | custom-call | tf_op jit(solution)/shard_map/update/pallas_call | solution.py:176
  32.9 0.4 collective-permute-start.10
  33.3 1.2 %collective-permute-done.11.theirs = f32[384,192]{1,0:T(8,128)S(1)} collective-permute-done((f32[384,192]{1,0:T(8,128)S(1)}, f32[384,192]{1,0:T(8,128)S(1)}, u32[]{:S(2)}, u32[]{:S(2)}) %collective-permute-start.11) | collective-permute-done | bytes 294944 | tf_op jit(solution)/shard_map/ppermute | solution.py:42
  34.5 2.9 %gradient.1 = bf16[64,144,128]{2,1,0:T(8,128)(2,1)} custom-call(f32[384,192]{1,0:T(8,128)S(1)} %get-tuple-element.9.mine, f32[384,192]{1,0:T(8,128)S(1)} %collective-permute-done.11.theirs, bf16[192,192]{1,0:T(8,128)(2,1)S(1)} %copy-done.1, bf16[192,192]{1,0:T(8,128)(2,1)S(1)} %collective-permute-done.9.signal_other, ...), custom_call_target="tpu_custom_call" | custom-call | tf_op jit(solution)/shard_map/gradient/pallas_call | solution.py:220
  37.4 8.6 %all-to-all-start = ((bf16[64,144,128]{2,1,0:T(8,128)(2,1)}), bf16[64,144,128]{2,1,0:T(8,128)(2,1)S(1)}, u32[]{:S(2)}, u32[]{:S(2)}) async-start(bf16[64,144,128]{2,1,0:T(8,128)(2,1)} %gradient.1), calls=%async_computation | async-start | bytes 4718592 | tf_op jit(solution)/shard_map/all_to_all | solution.py:315
  46.0 3.1 %place.1 = bf16[192,12288]{1,0:T(8,128)(2,1)} custom-call(s32[1]{0:T(128)} %bitcast.core, bf16[192,6144]{1,0:T(8,128)(2,1)} %collective-permute-done.10.fresh_back, bf16[192,12288]{1,0:T(8,128)(2,1)} %get-tuple-element.8.codes), custom_call_target="tpu_custom_call", output_to_operand_aliasing={{}: (2, {})} | custom-call | tf_op jit(solution)/shard_map/place/pallas_call | solution.py:244
  49.2 28.6 %all-to-all-done.pieces = bf16[64,144,128]{2,1,0:T(8,128)(2,1)S(1)} async-done(((bf16[64,144,128]{2,1,0:T(8,128)(2,1)}), bf16[64,144,128]{2,1,0:T(8,128)(2,1)S(1)}, u32[]{:S(2)}, u32[]{:S(2)}) %all-to-all-start) | async-done | bytes 2359328 | tf_op jit(solution)/shard_map/all_to_all | solution.py:315
  77.8 1.0 %finish.1 = f32[96,192]{1,0:T(8,128)} custom-call(bf16[64,144,128]{2,1,0:T(8,128)(2,1)S(1)} %all-to-all-done.pieces), custom_call_target="tpu_custom_call" | custom-call | tf_op jit(solution)/shard_map/finish/pallas_call | solution.py:268
  (15 shorter events, 1.2 us)
Async XLA Ops:
  0.6 1.8 %copy-start = (bf16[768,192]{0,1:T(8,128)(2,1)S(1)}, bf16[768,192]{0,1:T(8,128)(2,1)}, u32[]{:S(2)}) copy-start(bf16[768,192]{0,1:T(8,128)(2,1)} %param.5) | copy-start | bytes 884740
  2.4 17.8 %collective-permute-start = (bf16[192,6144]{1,0:T(8,128)(2,1)S(1)}, bf16[192,6144]{1,0:T(8,128)(2,1)S(1)}, u32[]{:S(2)}, u32[]{:S(2)}) collective-permute-start(bf16[192,6144]{1,0:T(8,128)(2,1)S(1)} %take.3), channel_id=1, source_target_pairs={{0,8},{8,0},{1,9},{9,1},{2,10},{10,2},{3,11},{11,3},{4,12},{12,4},... | collective-permute-start | bytes 7077896 | tf_op jit(solution)/shard_map/ppermute | solution.py:42
  2.5 8.0 %collective-permute-start.1 = (bf16[192,768]{1,0:T(8,128)(2,1)S(1)}, bf16[192,768]{1,0:T(8,128)(2,1)S(1)}, u32[]{:S(2)}, u32[]{:S(2)}) collective-permute-start(bf16[192,768]{1,0:T(8,128)(2,1)S(1)} %bitcast.4), channel_id=1, source_target_pairs={{0,16},{8,56},{16,32},{24,8},{32,48},{40,24},{48,0},{56,40},{64,80... | collective-permute-start | bytes 884744 | tf_op jit(solution)/shard_map/ppermute | solution.py:38
  4.1 10.5 %collective-permute-start.3 = (bf16[192,768]{1,0:T(8,128)(2,1)S(1)}, bf16[192,768]{1,0:T(8,128)(2,1)S(1)}, u32[]{:S(2)}, u32[]{:S(2)}) collective-permute-start(bf16[192,768]{1,0:T(8,128)(2,1)S(1)} %bitcast.5), channel_id=1, source_target_pairs={{0,64},{8,76},{16,80},{24,92},{32,96},{40,108},{48,112},{56,124},{... | collective-permute-start | bytes 884744 | tf_op jit(solution)/shard_map/ppermute | solution.py:38
  6.1 10.5 %collective-permute-start.2 = (bf16[192,768]{1,0:T(8,128)(2,1)S(1)}, bf16[192,768]{1,0:T(8,128)(2,1)S(1)}, u32[]{:S(2)}, u32[]{:S(2)}) collective-permute-start(bf16[192,768]{1,0:T(8,128)(2,1)S(1)} %bitcast.6), channel_id=1, source_target_pairs={{0,48},{8,24},{16,0},{24,40},{32,16},{40,56},{48,32},{56,8},{64,11... | collective-permute-start | bytes 884744 | tf_op jit(solution)/shard_map/ppermute | solution.py:38
  7.8 13.2 %collective-permute-start.6 = (bf16[192,768]{1,0:T(8,128)(2,1)S(1)}, bf16[192,768]{1,0:T(8,128)(2,1)S(1)}, u32[]{:S(2)}, u32[]{:S(2)}) collective-permute-start(bf16[192,768]{1,0:T(8,128)(2,1)S(1)} %bitcast.7), channel_id=1, source_target_pairs={{0,80},{8,124},{16,96},{24,76},{32,112},{40,92},{48,64},{56,108},{... | collective-permute-start | bytes 884744 | tf_op jit(solution)/shard_map/ppermute | solution.py:38
  10.5 13.2 %collective-permute-start.5 = (bf16[192,768]{1,0:T(8,128)(2,1)S(1)}, bf16[192,768]{1,0:T(8,128)(2,1)S(1)}, u32[]{:S(2)}, u32[]{:S(2)}) collective-permute-start(bf16[192,768]{1,0:T(8,128)(2,1)S(1)} %collective-permute-done.1.refs_1_), channel_id=1, source_target_pairs={{0,80},{8,124},{16,96},{24,76},{32,112},{40,92},{48,64},{56,108},{... | collective-permute-start | bytes 884744 | tf_op jit(solution)/shard_map/ppermute | solution.py:38
  14.7 11.1 %collective-permute-start.4 = (bf16[192,768]{1,0:T(8,128)(2,1)S(1)}, bf16[192,768]{1,0:T(8,128)(2,1)S(1)}, u32[]{:S(2)}, u32[]{:S(2)}) collective-permute-start(bf16[192,768]{1,0:T(8,128)(2,1)S(1)} %collective-permute-done.1.refs_1_), channel_id=1, source_target_pairs={{0,16},{8,56},{16,32},{24,8},{32,48},{40,24},{48,0},{56,40},{64,80... | collective-permute-start | bytes 884744 | tf_op jit(solution)/shard_map/ppermute | solution.py:38
  16.6 10.1 %collective-permute-start.7 = (bf16[192,768]{1,0:T(8,128)(2,1)S(1)}, bf16[192,768]{1,0:T(8,128)(2,1)S(1)}, u32[]{:S(2)}, u32[]{:S(2)}) collective-permute-start(bf16[192,768]{1,0:T(8,128)(2,1)S(1)} %collective-permute-done.2.refs_2_), channel_id=1, source_target_pairs={{0,64},{8,76},{16,80},{24,92},{32,96},{40,108},{48,112},{56,124},{... | collective-permute-start | bytes 884744 | tf_op jit(solution)/shard_map/ppermute | solution.py:38
  26.4 0.9 %copy-start.1 = (bf16[192,192]{1,0:T(8,128)(2,1)S(1)}, bf16[192,192]{1,0:T(8,128)(2,1)}, u32[]{:S(2)}) copy-start(bf16[192,192]{1,0:T(8,128)(2,1)} %signal_own.3) | copy-start | bytes 221188
  27.0 1.9 %collective-permute-start.8 = (f32[384,192]{1,0:T(8,128)S(1)}, f32[384,192]{1,0:T(8,128)S(1)}, u32[]{:S(2)}, u32[]{:S(2)}) collective-permute-start(f32[384,192]{1,0:T(8,128)S(1)} %estimate.5.mine), channel_id=1, source_target_pairs={{0,8},{8,0},{1,9},{9,1},{2,10},{10,2},{3,11},{11,3},{4,12},{12,4},... | collective-permute-start | bytes 884744 | tf_op jit(solution)/shard_map/ppermute | solution.py:42
  27.3 1.7 %collective-permute-start.9 = (bf16[192,192]{1,0:T(8,128)(2,1)S(1)}, bf16[192,192]{1,0:T(8,128)(2,1)S(1)}, u32[]{:S(2)}, u32[]{:S(2)}) collective-permute-start(bf16[192,192]{1,0:T(8,128)(2,1)S(1)} %copy-done.1), channel_id=1, source_target_pairs={{0,8},{8,0},{1,9},{9,1},{2,10},{10,2},{3,11},{11,3},{4,12},{12,4},... | collective-permute-start | bytes 221192 | tf_op jit(solution)/shard_map/ppermute | solution.py:42
  32.7 1.8 %collective-permute-start.11 = (f32[384,192]{1,0:T(8,128)S(1)}, f32[384,192]{1,0:T(8,128)S(1)}, u32[]{:S(2)}, u32[]{:S(2)}) collective-permute-start(f32[384,192]{1,0:T(8,128)S(1)} %get-tuple-element.9.mine), channel_id=1, source_target_pairs={{0,8},{8,0},{1,9},{9,1},{2,10},{10,2},{3,11},{11,3},{4,12},{12,4},... | collective-permute-start | bytes 884744 | tf_op jit(solution)/shard_map/ppermute | solution.py:42
  32.9 13.1 %collective-permute-start.10 = (bf16[192,6144]{1,0:T(8,128)(2,1)}, bf16[192,6144]{1,0:T(8,128)(2,1)}, u32[]{:S(2)}, u32[]{:S(2)}) collective-permute-start(bf16[192,6144]{1,0:T(8,128)(2,1)} %get-tuple-element.7), channel_id=1, source_target_pairs={{0,8},{8,0},{1,9},{9,1},{2,10},{10,2},{3,11},{11,3},{4,12},{12,4},... | collective-permute-start | bytes 7077896 | tf_op jit(solution)/shard_map/ppermute | solution.py:42
  37.4 40.4 %all-to-all-start = ((bf16[64,144,128]{2,1,0:T(8,128)(2,1)}), bf16[64,144,128]{2,1,0:T(8,128)(2,1)S(1)}, u32[]{:S(2)}, u32[]{:S(2)}) async-start(bf16[64,144,128]{2,1,0:T(8,128)(2,1)} %gradient.1), calls=%async_computation | async-start | bytes 4718592 | tf_op jit(solution)/shard_map/all_to_all | solution.py:315
where the time goes:
time: 80.3 us; the launch traced here: 78.8 us
  waiting for transfers between devices  37.2 us (46%)
  starting transfers between devices  24.7 us (31%)
  Pallas kernels  15.9 us (20%)
    all_to_all x1, waiting for transfers between devices, step(): functools.partial(lax.all_to_all, tiled=True)  28.6 us
    ppermute x7, starting transfers between devices, send(): return lax.ppermute(value, ('z_lo', 'x', 'core', 'z_hi'), pairs)  15 us
    all_to_all x1, starting transfers between devices, step(): functools.partial(lax.all_to_all, tiled=True)  8.6 us
    ppermute x7, waiting for transfers between devices, send(): return lax.ppermute(value, ('z_lo', 'x', 'core', 'z_hi'), pairs)  6.03 us
    pallas_call x1, Pallas kernels, update(): pl.pallas_call(functools.partial(update_kernel, shifts, counts), out_shap...  3.68 us
    pallas_call x2, Pallas kernels, take_half(): pl.pallas_call(functools.partial(take_kernel, flip), out_shape=pltpu.VMEM...  3.37 us
    pallas_call x1, Pallas kernels, place(): pl.pallas_call(place_kernel, out_shape=pltpu.HBM(codes.shape, BF16), in_s...  3.13 us
    pallas_call x1, Pallas kernels, gradient(): pl.pallas_call(gradient_kernel, out_shape=pltpu.HBM(pieces, BF16), in_spe...  2.94 us
  transfers between devices with their start and end apart: 13, of which 7 were waited for; matrix products, arithmetic and copies ran while one was open for 0% of the time, Pallas kernels for 12%

commit v1 on v0

--- a/solution.py
+++ b/solution.py
@@ -206,9 +206,11 @@
             buf[q * 8 + n, 0:part] = piece[:, 0:128].astype(BF16)
             tail = jnp.where(low, piece[: part // 2, 128:256], piece[part // 2 :, 128:256])
             buf[q * 8 + n, part : part + part // 2] = tail.astype(BF16)
-        copy = pltpu.make_async_copy(buf.at[q * 8 : q * 8 + 8], out.at[q * 8 : q * 8 + 8], sems.at[q])
-        copy.start()
-        copies.append(copy)
+            if n % 4 == 3:
+                span = slice(q * 8 + n - 3, q * 8 + n + 1)
+                copy = pltpu.make_async_copy(buf.at[span], out.at[span], sems.at[q, n // 4])
+                copy.start()
+                copies.append(copy)
     for copy in copies:
         copy.wait()
 
@@ -222,7 +224,7 @@
         out_shape=pltpu.HBM(pieces, BF16),
         in_specs=[VMEM] * 6,
         out_specs=ANY,
-        scratch_shapes=[pltpu.VMEM(pieces, BF16), pltpu.SemaphoreType.DMA((8,))],
+        scratch_shapes=[pltpu.VMEM(pieces, BF16), pltpu.SemaphoreType.DMA((8, 2))],
         compiler_params=PARAMS,
         name="gradient",
     )(*[near_memory(v) for v in given])

time: 80.3 us -> 80.3 us (level)
  no operation moved by 1% of the time
where the time goes in v1:
time: 80.3 us; the launch traced here: 78.8 us
  waiting for transfers between devices  37.3 us (46%)
  starting transfers between devices  24.6 us (31%)
  Pallas kernels  15.9 us (20%)
    all_to_all x1, waiting for transfers between devices, step(): functools.partial(lax.all_to_all, tiled=True)  28.6 us
    ppermute x7, starting transfers between devices, send(): return lax.ppermute(value, ('z_lo', 'x', 'core', 'z_hi'), pairs)  15 us
    all_to_all x1, starting transfers between devices, step(): functools.partial(lax.all_to_all, tiled=True)  8.59 us
    ppermute x7, waiting for transfers between devices, send(): return lax.ppermute(value, ('z_lo', 'x', 'core', 'z_hi'), pairs)  6.03 us
    pallas_call x1, Pallas kernels, update(): pl.pallas_call(functools.partial(update_kernel, shifts, counts), out_shap...  3.68 us
    pallas_call x2, Pallas kernels, take_half(): pl.pallas_call(functools.partial(take_kernel, flip), out_shape=pltpu.VMEM...  3.37 us
    pallas_call x1, Pallas kernels, place(): pl.pallas_call(place_kernel, out_shape=pltpu.HBM(codes.shape, BF16), in_s...  3.13 us
    pallas_call x1, Pallas kernels, gradient(): pl.pallas_call(gradient_kernel, out_shape=pltpu.HBM(pieces, BF16), in_spe...  2.94 us
  transfers between devices with their start and end apart: 13, of which 7 were waited for; matrix products, arithmetic and copies ran while one was open for 0% of the time, Pallas kernels for 12%

profile of v1, /device:TPU:0, one launch (start us, length us, event | category | flops | bytes accessed | tf_op | source)
XLA Modules:
  0.0 78.8 jit_solution(2863403543156502675)
XLA Ops:
  0.6 1.7 %take.3 = bf16[192,6144]{1,0:T(8,128)(2,1)S(1)} custom-call(s32[1]{0:T(128)} %bitcast.core, s32[1]{0:T(128)} %bitcast.1.x, s32[1]{0:T(128)} %bitcast.2.z_lo, bf16[192,12288]{1,0:T(8,128)(2,1)} %codes.3), custom_call_target="tpu_custom_call" | custom-call | tf_op jit(solution)/shard_map/take/pallas_call | solution.py:69
  2.5 1.7 %collective-permute-start.1 = (bf16[192,768]{1,0:T(8,128)(2,1)S(1)}, bf16[192,768]{1,0:T(8,128)(2,1)S(1)}, u32[]{:S(2)}, u32[]{:S(2)}) collective-permute-start(bf16[192,768]{1,0:T(8,128)(2,1)S(1)} %bitcast.4), channel_id=1, source_target_pairs={{0,16},{8,56},{16,32},{24,8},{32,48},{40,24},{48,0},{56,40},{64,80... | collective-permute-start | bytes 884744 | tf_op jit(solution)/shard_map/ppermute | solution.py:38
  4.1 1.9 %collective-permute-start.3 = (bf16[192,768]{1,0:T(8,128)(2,1)S(1)}, bf16[192,768]{1,0:T(8,128)(2,1)S(1)}, u32[]{:S(2)}, u32[]{:S(2)}) collective-permute-start(bf16[192,768]{1,0:T(8,128)(2,1)S(1)} %bitcast.5), channel_id=1, source_target_pairs={{0,64},{8,76},{16,80},{24,92},{32,96},{40,108},{48,112},{56,124},{... | collective-permute-start | bytes 884744 | tf_op jit(solution)/shard_map/ppermute | solution.py:38
  6.1 1.7 %collective-permute-start.2 = (bf16[192,768]{1,0:T(8,128)(2,1)S(1)}, bf16[192,768]{1,0:T(8,128)(2,1)S(1)}, u32[]{:S(2)}, u32[]{:S(2)}) collective-permute-start(bf16[192,768]{1,0:T(8,128)(2,1)S(1)} %bitcast.6), channel_id=1, source_target_pairs={{0,48},{8,24},{16,0},{24,40},{32,16},{40,56},{48,32},{56,8},{64,11... | collective-permute-start | bytes 884744 | tf_op jit(solution)/shard_map/ppermute | solution.py:38
  7.8 1.6 %collective-permute-start.6 = (bf16[192,768]{1,0:T(8,128)(2,1)S(1)}, bf16[192,768]{1,0:T(8,128)(2,1)S(1)}, u32[]{:S(2)}, u32[]{:S(2)}) collective-permute-start(bf16[192,768]{1,0:T(8,128)(2,1)S(1)} %bitcast.7), channel_id=1, source_target_pairs={{0,80},{8,124},{16,96},{24,76},{32,112},{40,92},{48,64},{56,108},{... | collective-permute-start | bytes 884744 | tf_op jit(solution)/shard_map/ppermute | solution.py:38
  9.4 1.0 %collective-permute-done.1.refs_1_ = bf16[192,768]{1,0:T(8,128)(2,1)S(1)} collective-permute-done((bf16[192,768]{1,0:T(8,128)(2,1)S(1)}, bf16[192,768]{1,0:T(8,128)(2,1)S(1)}, u32[]{:S(2)}, u32[]{:S(2)}) %collective-permute-start.1) | collective-permute-done | bytes 294944 | tf_op jit(solution)/shard_map/ppermute | solution.py:38
  10.5 4.2 %collective-permute-start.5 = (bf16[192,768]{1,0:T(8,128)(2,1)S(1)}, bf16[192,768]{1,0:T(8,128)(2,1)S(1)}, u32[]{:S(2)}, u32[]{:S(2)}) collective-permute-start(bf16[192,768]{1,0:T(8,128)(2,1)S(1)} %collective-permute-done.1.refs_1_), channel_id=1, source_target_pairs={{0,80},{8,124},{16,96},{24,76},{32,112},{40,92},{48,64},{56,108},{... | collective-permute-start | bytes 884744 | tf_op jit(solution)/shard_map/ppermute | solution.py:38
  14.7 1.9 %collective-permute-start.4 = (bf16[192,768]{1,0:T(8,128)(2,1)S(1)}, bf16[192,768]{1,0:T(8,128)(2,1)S(1)}, u32[]{:S(2)}, u32[]{:S(2)}) collective-permute-start(bf16[192,768]{1,0:T(8,128)(2,1)S(1)} %collective-permute-done.1.refs_1_), channel_id=1, source_target_pairs={{0,16},{8,56},{16,32},{24,8},{32,48},{40,24},{48,0},{56,40},{64,80... | collective-permute-start | bytes 884744 | tf_op jit(solution)/shard_map/ppermute | solution.py:38
  16.6 1.9 %collective-permute-start.7 = (bf16[192,768]{1,0:T(8,128)(2,1)S(1)}, bf16[192,768]{1,0:T(8,128)(2,1)S(1)}, u32[]{:S(2)}, u32[]{:S(2)}) collective-permute-start(bf16[192,768]{1,0:T(8,128)(2,1)S(1)} %collective-permute-done.2.refs_2_), channel_id=1, source_target_pairs={{0,64},{8,76},{16,80},{24,92},{32,96},{40,108},{48,112},{56,124},{... | collective-permute-start | bytes 884744 | tf_op jit(solution)/shard_map/ppermute | solution.py:38
  18.5 1.7 %take.2.own = bf16[192,6144]{1,0:T(8,128)(2,1)S(1)} custom-call(s32[1]{0:T(128)} %bitcast.core, s32[1]{0:T(128)} %bitcast.1.x, s32[1]{0:T(128)} %bitcast.2.z_lo, bf16[192,12288]{1,0:T(8,128)(2,1)} %codes.3), custom_call_target="tpu_custom_call" | custom-call | tf_op jit(solution)/shard_map/take/pallas_call | solution.py:69
  20.2 0.8 %estimate.3.refs_0_ = f32[384,192]{1,0:T(8,128)S(1)} custom-call(s32[1]{0:T(128)} %bitcast.core, s32[1]{0:T(128)} %bitcast.1.x, s32[1]{0:T(128)} %bitcast.2.z_lo, bf16[192,6144]{1,0:T(8,128)(2,1)S(1)} %take.2.own, bf16[192,6144]{1,0:T(8,128)(2,1)S(1)} %collective-permute-done.other, bf16[192,768]{1,0:T(8,128)(2,1)S(1)} %bitcast.8, ...), custom_call_target="tpu_custom_call" | custom-call | tf_op jit(solution)/shard_map/estimate/pallas_call | solution.py:122
  21.0 2.6 %collective-permute-done.5.refs_2_.refs_5_ = bf16[192,768]{1,0:T(8,128)(2,1)S(1)} collective-permute-done((bf16[192,768]{1,0:T(8,128)(2,1)S(1)}, bf16[192,768]{1,0:T(8,128)(2,1)S(1)}, u32[]{:S(2)}, u32[]{:S(2)}) %collective-permute-start.5) | collective-permute-done | bytes 294944 | tf_op jit(solution)/shard_map/ppermute | solution.py:38
  23.6 2.1 %collective-permute-done.4.refs_1_.refs_4_ = bf16[192,768]{1,0:T(8,128)(2,1)S(1)} collective-permute-done((bf16[192,768]{1,0:T(8,128)(2,1)S(1)}, bf16[192,768]{1,0:T(8,128)(2,1)S(1)}, u32[]{:S(2)}, u32[]{:S(2)}) %collective-permute-start.4) | collective-permute-done | bytes 294944 | tf_op jit(solution)/shard_map/ppermute | solution.py:38
  25.8 0.7 estimate.4.refs_0_
  26.7 0.3 estimate.5.mine
  27.6 1.4 %collective-permute-done.9.signal_other = bf16[192,192]{1,0:T(8,128)(2,1)S(1)} collective-permute-done((bf16[192,192]{1,0:T(8,128)(2,1)S(1)}, bf16[192,192]{1,0:T(8,128)(2,1)S(1)}, u32[]{:S(2)}, u32[]{:S(2)}) %collective-permute-start.9) | collective-permute-done | bytes 73760 | tf_op jit(solution)/shard_map/ppermute | solution.py:42
  29.0 3.7 %update.1 = (bf16[192,6144]{1,0:T(8,128)(2,1)S(1)}, bf16[192,6144]{1,0:T(8,128)(2,1)S(1)}, f32[384,192]{1,0:T(8,128)S(1)}, bf16[192,12288]{1,0:T(8,128)(2,1)}, bf16[192,6144]{1,0:T(8,128)(2,1)}) custom-call(s32[1]{0:T(128)} %bitcast.core, s32[1]{0:T(128)} %bitcast.1.x, s32[1]{0:T(128)} %bitcast.2.z_lo, bf16[192,6144]{1,0:T(8,128)(2,1)S(1)} %take.2.own, ...), custom_call_target="tpu_custom_call" | custom-call | tf_op jit(solution)/shard_map/update/pallas_call | solution.py:176
  32.9 0.4 collective-permute-start.10
  33.3 1.2 %collective-permute-done.11.theirs = f32[384,192]{1,0:T(8,128)S(1)} collective-permute-done((f32[384,192]{1,0:T(8,128)S(1)}, f32[384,192]{1,0:T(8,128)S(1)}, u32[]{:S(2)}, u32[]{:S(2)}) %collective-permute-start.11) | collective-permute-done | bytes 294944 | tf_op jit(solution)/shard_map/ppermute | solution.py:42
  34.5 2.9 %gradient.1 = bf16[64,144,128]{2,1,0:T(8,128)(2,1)} custom-call(f32[384,192]{1,0:T(8,128)S(1)} %get-tuple-element.9.mine, f32[384,192]{1,0:T(8,128)S(1)} %collective-permute-done.11.theirs, bf16[192,192]{1,0:T(8,128)(2,1)S(1)} %copy-done.1, bf16[192,192]{1,0:T(8,128)(2,1)S(1)} %collective-permute-done.9.signal_other, ...), custom_call_target="tpu_custom_call" | custom-call | tf_op jit(solution)/shard_map/gradient/pallas_call | solution.py:222
  37.4 8.6 %all-to-all-start = ((bf16[64,144,128]{2,1,0:T(8,128)(2,1)}), bf16[64,144,128]{2,1,0:T(8,128)(2,1)S(1)}, u32[]{:S(2)}, u32[]{:S(2)}) async-start(bf16[64,144,128]{2,1,0:T(8,128)(2,1)} %gradient.1), calls=%async_computation | async-start | bytes 4718592 | tf_op jit(solution)/shard_map/all_to_all | solution.py:317
  46.0 3.1 %place.1 = bf16[192,12288]{1,0:T(8,128)(2,1)} custom-call(s32[1]{0:T(128)} %bitcast.core, bf16[192,6144]{1,0:T(8,128)(2,1)} %collective-permute-done.10.fresh_back, bf16[192,12288]{1,0:T(8,128)(2,1)} %get-tuple-element.8.codes), custom_call_target="tpu_custom_call", output_to_operand_aliasing={{}: (2, {})} | custom-call | tf_op jit(solution)/shard_map/place/pallas_call | solution.py:246
  49.2 28.6 %all-to-all-done.pieces = bf16[64,144,128]{2,1,0:T(8,128)(2,1)S(1)} async-done(((bf16[64,144,128]{2,1,0:T(8,128)(2,1)}), bf16[64,144,128]{2,1,0:T(8,128)(2,1)S(1)}, u32[]{:S(2)}, u32[]{:S(2)}) %all-to-all-start) | async-done | bytes 2359328 | tf_op jit(solution)/shard_map/all_to_all | solution.py:317
  77.8 1.0 %finish.1 = f32[96,192]{1,0:T(8,128)} custom-call(bf16[64,144,128]{2,1,0:T(8,128)(2,1)S(1)} %all-to-all-done.pieces), custom_call_target="tpu_custom_call" | custom-call | tf_op jit(solution)/shard_map/finish/pallas_call | solution.py:270
  (15 shorter events, 1.2 us)
Async XLA Ops:
  0.6 1.8 %copy-start = (bf16[768,192]{0,1:T(8,128)(2,1)S(1)}, bf16[768,192]{0,1:T(8,128)(2,1)}, u32[]{:S(2)}) copy-start(bf16[768,192]{0,1:T(8,128)(2,1)} %param.5) | copy-start | bytes 884740
  2.4 17.8 %collective-permute-start = (bf16[192,6144]{1,0:T(8,128)(2,1)S(1)}, bf16[192,6144]{1,0:T(8,128)(2,1)S(1)}, u32[]{:S(2)}, u32[]{:S(2)}) collective-permute-start(bf16[192,6144]{1,0:T(8,128)(2,1)S(1)} %take.3), channel_id=1, source_target_pairs={{0,8},{8,0},{1,9},{9,1},{2,10},{10,2},{3,11},{11,3},{4,12},{12,4},... | collective-permute-start | bytes 7077896 | tf_op jit(solution)/shard_map/ppermute | solution.py:42
  2.5 8.0 %collective-permute-start.1 = (bf16[192,768]{1,0:T(8,128)(2,1)S(1)}, bf16[192,768]{1,0:T(8,128)(2,1)S(1)}, u32[]{:S(2)}, u32[]{:S(2)}) collective-permute-start(bf16[192,768]{1,0:T(8,128)(2,1)S(1)} %bitcast.4), channel_id=1, source_target_pairs={{0,16},{8,56},{16,32},{24,8},{32,48},{40,24},{48,0},{56,40},{64,80... | collective-permute-start | bytes 884744 | tf_op jit(solution)/shard_map/ppermute | solution.py:38
  4.1 10.5 %collective-permute-start.3 = (bf16[192,768]{1,0:T(8,128)(2,1)S(1)}, bf16[192,768]{1,0:T(8,128)(2,1)S(1)}, u32[]{:S(2)}, u32[]{:S(2)}) collective-permute-start(bf16[192,768]{1,0:T(8,128)(2,1)S(1)} %bitcast.5), channel_id=1, source_target_pairs={{0,64},{8,76},{16,80},{24,92},{32,96},{40,108},{48,112},{56,124},{... | collective-permute-start | bytes 884744 | tf_op jit(solution)/shard_map/ppermute | solution.py:38
  6.1 10.5 %collective-permute-start.2 = (bf16[192,768]{1,0:T(8,128)(2,1)S(1)}, bf16[192,768]{1,0:T(8,128)(2,1)S(1)}, u32[]{:S(2)}, u32[]{:S(2)}) collective-permute-start(bf16[192,768]{1,0:T(8,128)(2,1)S(1)} %bitcast.6), channel_id=1, source_target_pairs={{0,48},{8,24},{16,0},{24,40},{32,16},{40,56},{48,32},{56,8},{64,11... | collective-permute-start | bytes 884744 | tf_op jit(solution)/shard_map/ppermute | solution.py:38
  7.8 13.2 %collective-permute-start.6 = (bf16[192,768]{1,0:T(8,128)(2,1)S(1)}, bf16[192,768]{1,0:T(8,128)(2,1)S(1)}, u32[]{:S(2)}, u32[]{:S(2)}) collective-permute-start(bf16[192,768]{1,0:T(8,128)(2,1)S(1)} %bitcast.7), channel_id=1, source_target_pairs={{0,80},{8,124},{16,96},{24,76},{32,112},{40,92},{48,64},{56,108},{... | collective-permute-start | bytes 884744 | tf_op jit(solution)/shard_map/ppermute | solution.py:38
  10.5 13.2 %collective-permute-start.5 = (bf16[192,768]{1,0:T(8,128)(2,1)S(1)}, bf16[192,768]{1,0:T(8,128)(2,1)S(1)}, u32[]{:S(2)}, u32[]{:S(2)}) collective-permute-start(bf16[192,768]{1,0:T(8,128)(2,1)S(1)} %collective-permute-done.1.refs_1_), channel_id=1, source_target_pairs={{0,80},{8,124},{16,96},{24,76},{32,112},{40,92},{48,64},{56,108},{... | collective-permute-start | bytes 884744 | tf_op jit(solution)/shard_map/ppermute | solution.py:38
  14.7 11.1 %collective-permute-start.4 = (bf16[192,768]{1,0:T(8,128)(2,1)S(1)}, bf16[192,768]{1,0:T(8,128)(2,1)S(1)}, u32[]{:S(2)}, u32[]{:S(2)}) collective-permute-start(bf16[192,768]{1,0:T(8,128)(2,1)S(1)} %collective-permute-done.1.refs_1_), channel_id=1, source_target_pairs={{0,16},{8,56},{16,32},{24,8},{32,48},{40,24},{48,0},{56,40},{64,80... | collective-permute-start | bytes 884744 | tf_op jit(solution)/shard_map/ppermute | solution.py:38
  16.6 10.1 %collective-permute-start.7 = (bf16[192,768]{1,0:T(8,128)(2,1)S(1)}, bf16[192,768]{1,0:T(8,128)(2,1)S(1)}, u32[]{:S(2)}, u32[]{:S(2)}) collective-permute-start(bf16[192,768]{1,0:T(8,128)(2,1)S(1)} %collective-permute-done.2.refs_2_), channel_id=1, source_target_pairs={{0,64},{8,76},{16,80},{24,92},{32,96},{40,108},{48,112},{56,124},{... | collective-permute-start | bytes 884744 | tf_op jit(solution)/shard_map/ppermute | solution.py:38
  26.4 0.9 %copy-start.1 = (bf16[192,192]{1,0:T(8,128)(2,1)S(1)}, bf16[192,192]{1,0:T(8,128)(2,1)}, u32[]{:S(2)}) copy-start(bf16[192,192]{1,0:T(8,128)(2,1)} %signal_own.3) | copy-start | bytes 221188
  27.0 1.9 %collective-permute-start.8 = (f32[384,192]{1,0:T(8,128)S(1)}, f32[384,192]{1,0:T(8,128)S(1)}, u32[]{:S(2)}, u32[]{:S(2)}) collective-permute-start(f32[384,192]{1,0:T(8,128)S(1)} %estimate.5.mine), channel_id=1, source_target_pairs={{0,8},{8,0},{1,9},{9,1},{2,10},{10,2},{3,11},{11,3},{4,12},{12,4},... | collective-permute-start | bytes 884744 | tf_op jit(solution)/shard_map/ppermute | solution.py:42
  27.3 1.7 %collective-permute-start.9 = (bf16[192,192]{1,0:T(8,128)(2,1)S(1)}, bf16[192,192]{1,0:T(8,128)(2,1)S(1)}, u32[]{:S(2)}, u32[]{:S(2)}) collective-permute-start(bf16[192,192]{1,0:T(8,128)(2,1)S(1)} %copy-done.1), channel_id=1, source_target_pairs={{0,8},{8,0},{1,9},{9,1},{2,10},{10,2},{3,11},{11,3},{4,12},{12,4},... | collective-permute-start | bytes 221192 | tf_op jit(solution)/shard_map/ppermute | solution.py:42
  32.7 1.8 %collective-permute-start.11 = (f32[384,192]{1,0:T(8,128)S(1)}, f32[384,192]{1,0:T(8,128)S(1)}, u32[]{:S(2)}, u32[]{:S(2)}) collective-permute-start(f32[384,192]{1,0:T(8,128)S(1)} %get-tuple-element.9.mine), channel_id=1, source_target_pairs={{0,8},{8,0},{1,9},{9,1},{2,10},{10,2},{3,11},{11,3},{4,12},{12,4},... | collective-permute-start | bytes 884744 | tf_op jit(solution)/shard_map/ppermute | solution.py:42
  32.9 13.1 %collective-permute-start.10 = (bf16[192,6144]{1,0:T(8,128)(2,1)}, bf16[192,6144]{1,0:T(8,128)(2,1)}, u32[]{:S(2)}, u32[]{:S(2)}) collective-permute-start(bf16[192,6144]{1,0:T(8,128)(2,1)} %get-tuple-element.7), channel_id=1, source_target_pairs={{0,8},{8,0},{1,9},{9,1},{2,10},{10,2},{3,11},{11,3},{4,12},{12,4},... | collective-permute-start | bytes 7077896 | tf_op jit(solution)/shard_map/ppermute | solution.py:42
  37.4 40.4 %all-to-all-start = ((bf16[64,144,128]{2,1,0:T(8,128)(2,1)}), bf16[64,144,128]{2,1,0:T(8,128)(2,1)S(1)}, u32[]{:S(2)}, u32[]{:S(2)}) async-start(bf16[64,144,128]{2,1,0:T(8,128)(2,1)} %gradient.1), calls=%async_computation | async-start | bytes 4718592 | tf_op jit(solution)/shard_map/all_to_all | solution.py:317
